TPU v7x, 128 devices: a whole 4x4x4 slice. The times are simulated.
128 devices in a mesh: row: 8 (over z, core), col: 16 (over y, x).
Axes of the slice: x: 4, y: 4, z: 4, core: 2. Of those that a mesh axis runs over, the one named last changes fastest.
Arguments:
- snapshots: bfloat16 [4096, 32768], P('row', 'col'), may hold values from -14 to 14
- neighbours: int32 [4096, 128], P('row'), may hold values from 0 to 4095, all different within a row
- start_basis: float32 [32, 4096], replicated, may hold values from -6 to 6
Outputs:
- basis: float32 [32, 4096], P(None, 'row')
- rayleigh: float32 [32, 32], replicated
Inputs may be any that keep to these rules, and one draw needn't show every extreme that they name: `neighbours`: each row names 128 different snapshots.
All inputs are finite; a program needn't handle non-finite values.
Results may differ from a plain program's by a relative error of at most 0.00145.
Values may be sent and summed in bfloat16 or wider, within the bound.
No kernel may reach another device: no remote copies, remote signals or barrier semaphores. Data moves between devices by JAX's collectives and lax.ppermute only.
A program may use at most 128 MiB of HBM per device.

v0:
```python
import math
import jax
import jax.numpy as jnp
from jax import lax
from jax.sharding import PartitionSpec as P

FEATURES = 32768
LAGS = 64
ITERS = 2


def global_sum(value):
    return lax.psum(value, ("row", "col"))


def collect(columns):
    return lax.all_gather(columns, ("row", "col"), axis=1, tiled=True)


def shards(snapshots, neighbours, start_basis):
    row_count = lax.axis_size("row")
    col_count = lax.axis_size("col")
    row_at = lax.axis_index("row")
    col_at = lax.axis_index("col")
    lag_count = LAGS
    whole = lax.all_gather(snapshots, "row", axis=0, tiled=True)
    snap_count = whole.shape[0]
    feat_width = whole.shape[1]
    col_block = snap_count // col_count
    row_block = snapshots.shape[0]
    squares = jnp.sum(jnp.square(whole.astype(jnp.float32)), axis=1)
    padded_rows = jnp.concatenate([jnp.zeros((lag_count, feat_width), whole.dtype), whole], 0)
    padded_norms = jnp.concatenate([jnp.zeros((lag_count,), jnp.float32), squares], 0)
    row_start = row_at * row_block
    ext_rows = lax.dynamic_slice_in_dim(padded_rows, row_start, row_block + lag_count, 0)
    ext_norms = lax.dynamic_slice_in_dim(padded_norms, row_start, row_block + lag_count, 0)
    row_times = row_start - lag_count + jnp.arange(row_block + lag_count, dtype=jnp.int32)
    span = col_block + lag_count
    blocks = whole.reshape(col_count, col_block, feat_width)
    earlier = jnp.concatenate(
        [jnp.zeros((1, lag_count, feat_width), whole.dtype), blocks[:-1, col_block - lag_count :]],
        0,
    )
    source_rows = jnp.concatenate([earlier, blocks], 1).reshape(col_count * span, feat_width)
    norm_blocks = squares.reshape(col_count, col_block)
    norm_earlier = jnp.concatenate(
        [jnp.zeros((1, lag_count), jnp.float32), norm_blocks[:-1, col_block - lag_count :]], 0
    )
    source_norms = jnp.concatenate([norm_earlier, norm_blocks], 1).reshape(col_count * span)
    virtual = jnp.arange(span * lax.axis_size("col"), dtype=jnp.int32)
    times = virtual // span * col_block + virtual % span - lag_count
    inner = lax.dot_general(
        source_rows, ext_rows, (((1,), (1,)), ((), ())), preferred_element_type=jnp.float32
    )
    term = source_norms[:, None] + ext_norms[None, :] - 2.0 * inner
    keep = (times >= 0)[:, None] & (row_times >= 0)[None, :]
    tile = lax.psum_scatter(
        jnp.where(keep, term, 0.0).astype(jnp.bfloat16), "col", scatter_dimension=0, tiled=True
    ).astype(jnp.float32)
    window = 1
    while window < lag_count:
        tile = tile[window:, window:] + tile[:-window, :-window]
        window = window * 2
    lagged = tile[1:, 1:]
    step_rows = math.gcd(row_block, 16)
    block_count = row_block // step_rows
    slot_count = neighbours.shape[1]
    offset = neighbours - col_at * col_block
    inside = (offset >= 0) & (offset < col_block)
    tile_positions = jnp.arange(col_block, dtype=jnp.int32)

    def pick_block(pair):
        offs, lag_rows = pair
        match = offs[:, :, None] == tile_positions[None, None, :]
        return jnp.sum(jnp.where(match, lag_rows[:, None, :], 0.0), axis=2)

    chosen = lax.map(
        pick_block,
        (
            offset.reshape(block_count, step_rows, slot_count),
            lagged.T.reshape(block_count, step_rows, col_block),
        ),
    )
    chosen = chosen.reshape(row_block, slot_count)
    kernel_part = jnp.where(inside, 1.0 / (1.0 + chosen / (LAGS * FEATURES)), 0.0)
    slot_kernel = lax.psum(kernel_part, "col")
    mass = jnp.sum(slot_kernel, axis=1)
    markov = slot_kernel / mass[:, None]
    snap_positions = jnp.arange(snap_count, dtype=jnp.int32)

    def operator_block(pair):
        ids, weights = pair
        match = ids[:, :, None] == snap_positions[None, None, :]
        return jnp.sum(jnp.where(match, weights[:, :, None], 0.0), axis=1)

    transition = lax.map(
        operator_block,
        (
            neighbours.reshape(block_count, step_rows, slot_count),
            markov.reshape(block_count, step_rows, slot_count),
        ),
    )
    transition = transition.reshape(row_block, snap_count)
    piece_width = snap_count // (row_count * col_count)

    def apply_rows(basis_rows):
        return lax.dot_general(
            basis_rows,
            transition,
            (((1,), (1,)), ((), ())),
            precision=lax.Precision.HIGHEST,
            preferred_element_type=jnp.float32,
        )

    def own_piece(image):
        return lax.dynamic_slice_in_dim(image, col_at * piece_width, piece_width, 1)

    basis = start_basis
    for step in range(ITERS):
        piece = own_piece(apply_rows(basis))
        partial_gram = jnp.dot(
            piece, piece.T, precision=lax.Precision.HIGHEST, preferred_element_type=jnp.float32
        )
        gram_small = global_sum(partial_gram) / snap_count
        lower = jnp.linalg.cholesky(gram_small)
        basis = collect(jax.scipy.linalg.solve_triangular(lower, piece, lower=True))
    image_piece = own_piece(apply_rows(basis))
    basis_piece = lax.dynamic_slice_in_dim(
        basis, (row_at * col_count + col_at) * piece_width, piece_width, 1
    )
    partial_ray = jnp.dot(
        basis_piece,
        image_piece.T,
        precision=lax.Precision.HIGHEST,
        preferred_element_type=jnp.float32,
    )
    rayleigh = global_sum(partial_ray) / snap_count
    basis_rows = lax.dynamic_slice_in_dim(basis, row_start, row_block, 1)
    return (basis_rows, rayleigh)


def solution(mesh):
    placed = (P("row", "col"), P("row", None), P())
    return jax.shard_map(
        shards, mesh=mesh, in_specs=placed, out_specs=(P(None, "row"), P()), check_vma=False
    )
```

profile of v0, /device:TPU:1, one launch (start us, length us, event | category | flops | bytes accessed | tf_op | source)
XLA Modules:
  0.0 1007.9 jit_solution(16402256858035387622)
XLA Ops:
  8.0 90.6 %all-gather.2.cloned.1.call-done = bf16[4096,2048]{1,0:T(8,128)(2,1)} async-done(((bf16[512,2048]{1,0:T(8,128)(2,1)}), bf16[4096,2048]{1,0:T(8,128)(2,1)}) %all-gather.2.cloned.1.call-update) | async-done | bytes 16777232 | tf_op jit(solution)/shard_map/all_gather | solution.py:26
  108.7 21.4 %fusion.5 = bf16[16,320,2048]{2,1,0:T(8,128)(2,1)} fusion(bf16[15,64,2048]{2,1,0:T(8,128)(2,1)S(1)} %slice.69, bf16[16,256,2048]{2,1,0:T(8,128)(2,1)} %bitcast.64), kind=kLoop, calls=%fused_computation.15 | loop fusion | flops 62914560 | bytes 41680896 | tf_op jit(solution)/shard_map/concatenate | solution.py:44
  130.2 23.8 %select_convert_fusion = bf16[5120,576]{1,0:T(8,128)(2,1)} fusion(bf16[5120,2048]{1,0:T(8,128)(2,1)} %bitcast.70, f32[576]{0:T(1024)S(1)} %pad_dynamic-slice_fusion.2, f32[5120]{0:T(1024)S(1)} %add.130, pred[576]{0:T(1024)(128)(4,1)S(1)} %add_compare_fusion, pred[5120]{0:T(1024)(128)(4,1)S(1)} %fusion.17, s32[]{:T(128)S(6)} %select_n.56, ...), kind=kOutput, calls=%fused_computation.17 | convolution fusion | flops 12097290240 | bytes 43675460 | tf_op jit(solution)/shard_map/dot_general | solution.py:52
  154.1 80.7 %reduce-scatter.2.cloned.1.call-done = bf16[320,576]{1,0:T(8,128)(2,1)} async-done(((bf16[5120,576]{1,0:T(8,128)(2,1)}), bf16[320,576]{1,0:T(8,128)(2,1)}) %reduce-scatter.2.cloned.1.call-update) | async-done | bytes 368656 | tf_op jit(solution)/shard_map/reduce_scatter | solution.py:57
  238.1 28.1 %while.22 = (s32[]{:T(128)}, f32[32,16,128]{2,1,0:T(8,128)S(1)}, s32[32,16,128]{2,1,0:T(8,128)S(1)}, f32[32,16,256]{2,1,0:T(8,128)S(1)}, s32[]{:T(128)}) while((s32[]{:T(128)}, f32[32,16,128]{2,1,0:T(8,128)S(1)}, s32[32,16,128]{2,1,0:T(8,128)S(1)}, f32[32,16,256]{2,1,0:T(8,128)S(1)}, s32[]{:T(128)}) %tuple.63), condition=%wide.region_4.5_spmd.clone, body=%wide.region_2.4_spmd.clone.sunk | while | flops 1570818 | bytes 98377 | solution.py:77
  267.0 83.3 %all-reduce.6.cloned.1.call-done = f32[512,128]{1,0:T(8,128)} async-done(((f32[512,128]{1,0:T(8,128)}), f32[512,128]{1,0:T(8,128)}) %all-reduce.6.cloned.1.call-update) | async-done | bytes 262160 | tf_op jit(solution)/shard_map/psum | solution.py:86
  352.5 280.2 %while.23 = (s32[]{:T(128)}, f32[32,16,4096]{2,1,0:T(8,128)}, s32[32,16,128]{2,1,0:T(8,128)S(1)}, f32[32,16,128]{2,1,0:T(8,128)S(1)}, s32[]{:T(128)}) while((s32[]{:T(128)}, f32[32,16,4096]{2,1,0:T(8,128)}, s32[32,16,128]{2,1,0:T(8,128)S(1)}, f32[32,16,128]{2,1,0:T(8,128)S(1)}, s32[]{:T(128)}) %tuple.64), condition=%wide.region_9.10_spmd.clone, body=%wide.region_7.9_spmd.clone.sunk | while | flops 25100288 | bytes 836165 | solution.py:96
  361.3 8.0 select_reduce_fusion.6
  370.0 8.0 select_reduce_fusion.6
  378.8 8.0 select_reduce_fusion.6
  387.5 8.0 select_reduce_fusion.6
  396.3 8.0 select_reduce_fusion.6
  405.1 8.0 select_reduce_fusion.6
  413.8 8.0 select_reduce_fusion.6
  422.6 8.0 select_reduce_fusion.6
  431.4 8.0 select_reduce_fusion.6
  440.1 8.0 select_reduce_fusion.6
  448.9 8.0 select_reduce_fusion.6
  457.6 8.0 select_reduce_fusion.6
  466.4 8.0 select_reduce_fusion.6
  475.1 8.0 select_reduce_fusion.6
  483.9 8.0 select_reduce_fusion.6
  492.6 8.0 select_reduce_fusion.6
  501.4 8.0 select_reduce_fusion.6
  632.7 9.2 fusion.46
  642.1 65.8 %psum.29 = f32[32,32]{0,1:T(8,128)S(1)} all-reduce(f32[32,32]{0,1:T(8,128)S(1)} %fusion.36), channel_id=1, replica_groups=mesh['row'=8,'col'=16] {'row','col'}, use_global_device_ids=true, to_apply=%region_10.11 | all-reduce | flops 1024 | bytes 8192 | tf_op jit(solution)/shard_map/psum | solution.py:13
  714.8 63.7 %all_gather.10 = f32[32,4096]{0,1:T(8,128)S(1)} all-gather(f32[32,32]{0,1:T(8,128)S(1)} %fusion.23), channel_id=1, replica_groups=mesh['row'=8,'col'=16] {'row','col'}, dimensions={1}, use_global_device_ids=true | all-gather | bytes 528384 | tf_op jit(solution)/shard_map/all_gather | solution.py:17
  778.6 9.3 fusion.47
  788.1 65.0 %psum.30 = f32[32,32]{0,1:T(8,128)S(1)} all-reduce(f32[32,32]{0,1:T(8,128)S(1)} %fusion.33), channel_id=1, replica_groups=mesh['row'=8,'col'=16] {'row','col'}, use_global_device_ids=true, to_apply=%region_13.16 | all-reduce | flops 1024 | bytes 8192 | tf_op jit(solution)/shard_map/psum | solution.py:13
  860.2 65.1 %all_gather.11 = f32[32,4096]{0,1:T(8,128)S(1)} all-gather(f32[32,32]{0,1:T(8,128)S(1)} %fusion.20), channel_id=1, replica_groups=mesh['row'=8,'col'=16] {'row','col'}, dimensions={1}, use_global_device_ids=true | all-gather | bytes 528384 | tf_op jit(solution)/shard_map/all_gather | solution.py:17
  925.3 9.2 fusion.48
  934.8 65.0 %psum.31 = f32[32,32]{0,1:T(8,128)S(1)} all-reduce(f32[32,32]{0,1:T(8,128)S(1)} %fusion.29), channel_id=1, replica_groups=mesh['row'=8,'col'=16] {'row','col'}, use_global_device_ids=true, to_apply=%region_14.17 | all-reduce | flops 1024 | bytes 8192 | tf_op jit(solution)/shard_map/psum | solution.py:13
  (308 shorter events, 203.1 us)
Async XLA Ops:
  7.2 625.5 %copy-start = (f32[32,4096]{1,0:T(8,128)S(1)}, f32[32,4096]{1,0:T(8,128)}, u32[]{:S(2)}) copy-start(f32[32,4096]{1,0:T(8,128)} %param.12) | copy-start | bytes 1572868
  7.2 91.4 %all-gather.2.cloned.1.call-start = ((), (), s32[]{:S(2)}) async-start(), calls=%async_computation.1 | async-start | bytes 18874368 | tf_op jit(solution)/shard_map/all_gather | solution.py:26
  7.9 226.8 %reduce-scatter.2.cloned.1.call-start = ((), (), s32[]{:S(2)}) async-start(), calls=%async_computation.2 | async-start | bytes 6963200 | tf_op jit(solution)/shard_map/reduce_scatter | solution.py:57
  106.1 24.0 %slice-start = ((s8[16777216]{0:T(1024)(128)(4,1)}), s8[4194304]{0:T(1024)(128)(4,1)S(1)}, s32[]{:S(2)}) async-start(s8[16777216]{0:T(1024)(128)(4,1)} %bitcast.65), calls=%async_computation.4 | async-start | bytes 8388608
  108.7 21.5 %slice-start.1 = ((s8[16777216]{0:T(1024)(128)(4,1)}), s8[4194304]{0:T(1024)(128)(4,1)S(1)}, s32[]{:S(2)}) async-start(s8[16777216]{0:T(1024)(128)(4,1)} %bitcast.65), calls=%async_computation.5 | async-start | bytes 8388608
  108.7 21.4 %slice-start.2 = ((s8[16777216]{0:T(1024)(128)(4,1)}), s8[4194304]{0:T(1024)(128)(4,1)S(1)}, s32[]{:S(2)}) async-start(s8[16777216]{0:T(1024)(128)(4,1)} %bitcast.65), calls=%async_computation.6 | async-start | bytes 8388608
  108.7 21.4 %slice-start.3 = ((s8[16777216]{0:T(1024)(128)(4,1)}), s8[4194304]{0:T(1024)(128)(4,1)S(1)}, s32[]{:S(2)}) async-start(s8[16777216]{0:T(1024)(128)(4,1)} %bitcast.65), calls=%async_computation.7 | async-start | bytes 8388608
  130.1 23.9 %copy-start.1 = (s32[512,128]{1,0:T(8,128)S(1)}, s32[512,128]{1,0:T(8,128)}, u32[]{:S(2)}) copy-start(s32[512,128]{1,0:T(8,128)} %param.11) | copy-start | bytes 786436
  154.0 196.3 %all-reduce.6.cloned.1.call-start = ((), (), s32[]{:S(2)}) async-start(), calls=%async_computation.3 | async-start | bytes 524288 | tf_op jit(solution)/shard_map/psum | solution.py:86
Sparse Core Ops, SparseCore 0:
  9.7 88.8 all-gather.1
  154.1 80.6 reduce-scatter.1
  267.1 83.1 all-reduce.5
where the time goes:
time: 1020 us; the launch traced here: 1010 us
  other arithmetic  330 us (32%)
  blocking collectives  325 us (32%)
  waiting for transfers between devices  255 us (25%)
  matrix products  52.6 us (5%)
  local copies, waits for them, and re-layouts  29.2 us (3%)
  between operations  14.3 us (1%)
    reduce_sum x32, other arithmetic, operator_block(): return jnp.sum(jnp.where(match, weights[:, :, None], 0.0), axis=1)  256 us
    psum x3, blocking collectives, global_sum(): return lax.psum(value, ('row', 'col'))  196 us
    all_gather x2, blocking collectives, collect(): return lax.all_gather(columns, ('row', 'col'), axis=1, tiled=True)  129 us
    all_gather x1, waiting for transfers between devices, shards(): whole = lax.all_gather(snapshots, 'row', axis=0, tiled=True)  90.6 us
    psum x1, waiting for transfers between devices, shards(): slot_kernel = lax.psum(kernel_part, 'col')  83.3 us
    reduce_scatter x1, waiting for transfers between devices, shards(): lax.psum_scatter(jnp.where(keep, term, 0.0).astype(jnp.bfloat16), 'col',...  80.7 us
    dot_general x3, matrix products, apply_rows(): lax.dot_general(basis_rows, transition, (((1,), (1,)), ((), ())), precisi...  27.6 us
    reduce_sum x32, other arithmetic, pick_block(): return jnp.sum(jnp.where(match, lag_rows[:, None, :], 0.0), axis=2)  25.3 us
  transfers between devices with their start and end apart: 3, of which 3 were waited for; matrix products, arithmetic and copies ran while one was open for 0% of the time, Pallas kernels for 0%

commit v1 on v0

--- a/solution.py
+++ b/solution.py
@@ -23,7 +23,9 @@
     row_at = lax.axis_index("row")
     col_at = lax.axis_index("col")
     lag_count = LAGS
-    whole = lax.all_gather(snapshots, "row", axis=0, tiled=True)
+    whole = jnp.concatenate(
+        lax.all_to_all(jnp.stack([snapshots] * lax.axis_size("row")), "row", 0, 0), axis=0
+    )
     snap_count = whole.shape[0]
     feat_width = whole.shape[1]
     col_block = snap_count // col_count

time: 1020 us -> 1110 us (1.088)
  waiting for transfers between devices: 255 us -> 348 us
    all_to_all x0 -> x1, waiting for transfers between devices: none -> 183 us  [shards(): lax.all_to_all(jnp.stack([snapshots] * lax.axis_size('row')), 'row', 0, 0)]
    all_gather x1 -> x0, waiting for transfers between devices: 90.6 us -> none  [shards(): whole = lax.all_gather(snapshots, 'row', axis=0, tiled=True)]
where the time goes in v1:
time: 1110 us; the launch traced here: 1100 us
  waiting for transfers between devices  348 us (31%)
  blocking collectives  325 us (29%)
  other arithmetic  321 us (29%)
  matrix products  50.9 us (5%)
  local copies, waits for them, and re-layouts  36 us (3%)
  between operations  14.5 us (1%)
    reduce_sum x32, other arithmetic, operator_block(): return jnp.sum(jnp.where(match, weights[:, :, None], 0.0), axis=1)  256 us
    psum x3, blocking collectives, global_sum(): return lax.psum(value, ('row', 'col'))  196 us
    all_to_all x1, waiting for transfers between devices, shards(): lax.all_to_all(jnp.stack([snapshots] * lax.axis_size('row')), 'row', 0, 0)  183 us
    all_gather x2, blocking collectives, collect(): return lax.all_gather(columns, ('row', 'col'), axis=1, tiled=True)  129 us
    psum x1, waiting for transfers between devices, shards(): slot_kernel = lax.psum(kernel_part, 'col')  83.3 us
    reduce_scatter x1, waiting for transfers between devices, shards(): lax.psum_scatter(jnp.where(keep, term, 0.0).astype(jnp.bfloat16), 'col',...  80.9 us
    dot_general x3, matrix products, apply_rows(): lax.dot_general(basis_rows, transition, (((1,), (1,)), ((), ())), precisi...  27.6 us
    reduce_sum x32, other arithmetic, pick_block(): return jnp.sum(jnp.where(match, lag_rows[:, None, :], 0.0), axis=2)  25.3 us
  transfers between devices with their start and end apart: 3, of which 3 were waited for; matrix products, arithmetic and copies ran while one was open for 0% of the time, Pallas kernels for 0%

profile of v1, /device:TPU:1, one launch (start us, length us, event | category | flops | bytes accessed | tf_op | source)
XLA Modules:
  0.0 1103.7 jit_solution(4570583440719818231)
XLA Ops:
  21.2 183.3 %all-to-all-done = bf16[8,512,2048]{2,1,0:T(8,128)(2,1)} async-done(((bf16[8,512,2048]{2,1,0:T(8,128)(2,1)}), bf16[8,512,2048]{2,1,0:T(8,128)(2,1)}, u32[]{:S(2)}, u32[]{:S(2)}) %all-to-all-start) | async-done | bytes 16777248 | tf_op jit(solution)/shard_map/all_to_all | solution.py:27
  214.4 13.2 %fusion.5 = bf16[16,320,2048]{2,1,0:T(8,128)(2,1)S(1)} fusion(bf16[15,64,2048]{2,1,0:T(8,128)(2,1)S(1)} %slice.69, bf16[16,256,2048]{2,1,0:T(8,128)(2,1)} %bitcast.2), kind=kLoop, calls=%fused_computation.15 | loop fusion | flops 62914560 | bytes 41680896 | tf_op jit(solution)/shard_map/concatenate | solution.py:46
  227.7 22.2 %select_convert_fusion = bf16[5120,576]{1,0:T(8,128)(2,1)} fusion(bf16[5120,2048]{1,0:T(8,128)(2,1)S(1)} %bitcast.69, f32[576]{0:T(1024)S(1)} %pad_dynamic-slice_fusion.2, f32[5120]{0:T(1024)S(1)} %add.130, pred[576]{0:T(1024)(128)(4,1)S(1)} %add_compare_fusion, pred[5120]{0:T(1024)(128)(4,1)S(1)} %fusion.17, s32[]{:T(128)S(6)} %select_n.56, ...), kind=kOutput, calls=%fused_computation.17 | convolution fusion | flops 12097290240 | bytes 43675460 | tf_op jit(solution)/shard_map/dot_general | solution.py:54
  250.0 80.9 %reduce-scatter.2.cloned.1.call-done = bf16[320,576]{1,0:T(8,128)(2,1)} async-done(((bf16[5120,576]{1,0:T(8,128)(2,1)}), bf16[320,576]{1,0:T(8,128)(2,1)}) %reduce-scatter.2.cloned.1.call-update) | async-done | bytes 368656 | tf_op jit(solution)/shard_map/reduce_scatter | solution.py:59
  334.3 28.1 %while.22 = (s32[]{:T(128)}, f32[32,16,128]{2,1,0:T(8,128)S(1)}, s32[32,16,128]{2,1,0:T(8,128)S(1)}, f32[32,16,256]{2,1,0:T(8,128)S(1)}, s32[]{:T(128)}) while((s32[]{:T(128)}, f32[32,16,128]{2,1,0:T(8,128)S(1)}, s32[32,16,128]{2,1,0:T(8,128)S(1)}, f32[32,16,256]{2,1,0:T(8,128)S(1)}, s32[]{:T(128)}) %tuple.61), condition=%wide.region_4.5_spmd.clone, body=%wide.region_2.4_spmd.clone.sunk | while | flops 1570818 | bytes 98377 | solution.py:79
  363.2 83.3 %all-reduce.6.cloned.1.call-done = f32[512,128]{1,0:T(8,128)} async-done(((f32[512,128]{1,0:T(8,128)}), f32[512,128]{1,0:T(8,128)}) %all-reduce.6.cloned.1.call-update) | async-done | bytes 262160 | tf_op jit(solution)/shard_map/psum | solution.py:88
  448.7 279.5 %while.23 = (s32[]{:T(128)}, f32[32,16,4096]{2,1,0:T(8,128)}, s32[32,16,128]{2,1,0:T(8,128)S(1)}, f32[32,16,128]{2,1,0:T(8,128)S(1)}, s32[]{:T(128)}) while((s32[]{:T(128)}, f32[32,16,4096]{2,1,0:T(8,128)}, s32[32,16,128]{2,1,0:T(8,128)S(1)}, f32[32,16,128]{2,1,0:T(8,128)S(1)}, s32[]{:T(128)}) %tuple.62), condition=%wide.region_9.10_spmd.clone, body=%wide.region_7.9_spmd.clone.sunk | while | flops 25100288 | bytes 836165 | solution.py:98
  457.5 8.0 select_reduce_fusion.6
  474.9 8.0 select_reduce_fusion.6
  483.7 8.0 select_reduce_fusion.6
  509.9 8.0 select_reduce_fusion.6
  518.6 8.0 select_reduce_fusion.6
  527.4 8.0 select_reduce_fusion.6
  544.8 8.0 select_reduce_fusion.6
  553.6 8.0 select_reduce_fusion.6
  562.3 8.0 select_reduce_fusion.6
  571.0 8.0 select_reduce_fusion.6
  597.2 8.0 select_reduce_fusion.6
  632.2 8.0 select_reduce_fusion.6
  640.9 8.0 select_reduce_fusion.6
  649.6 8.0 select_reduce_fusion.6
  658.4 8.0 select_reduce_fusion.6
  667.1 8.0 select_reduce_fusion.6
  675.9 8.0 select_reduce_fusion.6
  728.2 9.2 fusion.46
  737.6 65.8 %psum.29 = f32[32,32]{0,1:T(8,128)S(1)} all-reduce(f32[32,32]{0,1:T(8,128)S(1)} %fusion.36), channel_id=1, replica_groups=mesh['row'=8,'col'=16] {'row','col'}, use_global_device_ids=true, to_apply=%region_10.11 | all-reduce | flops 1024 | bytes 8192 | tf_op jit(solution)/shard_map/psum | solution.py:13
  810.4 63.7 %all_gather.6 = f32[32,4096]{0,1:T(8,128)S(1)} all-gather(f32[32,32]{0,1:T(8,128)S(1)} %fusion.23), channel_id=1, replica_groups=mesh['row'=8,'col'=16] {'row','col'}, dimensions={1}, use_global_device_ids=true | all-gather | bytes 528384 | tf_op jit(solution)/shard_map/all_gather | solution.py:17
  874.1 9.3 fusion.47
  883.6 65.0 %psum.30 = f32[32,32]{0,1:T(8,128)S(1)} all-reduce(f32[32,32]{0,1:T(8,128)S(1)} %fusion.33), channel_id=1, replica_groups=mesh['row'=8,'col'=16] {'row','col'}, use_global_device_ids=true, to_apply=%region_13.16 | all-reduce | flops 1024 | bytes 8192 | tf_op jit(solution)/shard_map/psum | solution.py:13
  955.7 65.1 %all_gather.7 = f32[32,4096]{0,1:T(8,128)S(1)} all-gather(f32[32,32]{0,1:T(8,128)S(1)} %fusion.20), channel_id=1, replica_groups=mesh['row'=8,'col'=16] {'row','col'}, dimensions={1}, use_global_device_ids=true | all-gather | bytes 528384 | tf_op jit(solution)/shard_map/all_gather | solution.py:17
  1020.8 9.2 fusion.48
  1030.3 65.0 %psum.31 = f32[32,32]{0,1:T(8,128)S(1)} all-reduce(f32[32,32]{0,1:T(8,128)S(1)} %fusion.29), channel_id=1, replica_groups=mesh['row'=8,'col'=16] {'row','col'}, use_global_device_ids=true, to_apply=%region_14.17 | all-reduce | flops 1024 | bytes 8192 | tf_op jit(solution)/shard_map/psum | solution.py:13
  (300 shorter events, 215.9 us)
Async XLA Ops:
  7.2 721.1 %copy-start = (f32[32,4096]{1,0:T(8,128)S(1)}, f32[32,4096]{1,0:T(8,128)}, u32[]{:S(2)}) copy-start(f32[32,4096]{1,0:T(8,128)} %param.12) | copy-start | bytes 1572868
  14.1 190.4 %all-to-all-start = ((bf16[8,512,2048]{2,1,0:T(8,128)(2,1)}), bf16[8,512,2048]{2,1,0:T(8,128)(2,1)}, u32[]{:S(2)}, u32[]{:S(2)}) async-start(bf16[8,512,2048]{2,1,0:T(8,128)(2,1)} %stack.2), calls=%async_computation | async-start | bytes 33554432 | tf_op jit(solution)/shard_map/all_to_all | solution.py:27
  21.2 309.8 %reduce-scatter.2.cloned.1.call-start = ((), (), s32[]{:S(2)}) async-start(), calls=%async_computation.2 | async-start | bytes 6963200 | tf_op jit(solution)/shard_map/reduce_scatter | solution.py:59
  227.7 22.3 %copy-start.1 = (s32[512,128]{1,0:T(8,128)S(1)}, s32[512,128]{1,0:T(8,128)}, u32[]{:S(2)}) copy-start(s32[512,128]{1,0:T(8,128)} %param.11) | copy-start | bytes 786436
  249.9 196.6 %all-reduce.6.cloned.1.call-start = ((), (), s32[]{:S(2)}) async-start(), calls=%async_computation.3 | async-start | bytes 524288 | tf_op jit(solution)/shard_map/psum | solution.py:88
Sparse Core Ops, SparseCore 0:
  250.0 80.8 reduce-scatter.1
  363.3 83.1 all-reduce.5
